TPU v7x, 512 devices: a whole 4x8x8 slice. The times are simulated.
512 devices in a mesh: blk: 16 (over y, z_lo), wide: 32 (over x, z_hi, core).
Axes of the slice: x: 4, y: 8, z: 8 (z_hi: 4, z_lo: 2; z = z_hi * 2 + z_lo), core: 2. Of those that a mesh axis runs over, the one named last changes fastest.
Arguments:
- tokens: bfloat16 [24576, 128], P(('blk', 'wide')), may hold values from -11 to 11
- centroids: bfloat16 [131072, 128], P('blk'), may hold values from -7 to 7
- row_ids: int32 [512, 16, 32], P(('blk', 'wide')), may hold values from 0 to 47
- alt_ids: int32 [512, 16, 32], P(('blk', 'wide')), may hold values from 0 to 8191
- counts: int32 [512, 16], P(('blk', 'wide')), may hold values from 1 to 32, as said below
Outputs:
- row_duals: float32 [24576], P(('blk', 'wide'))
- col_duals: float32 [131072], P('blk')
- residuals: float32 [512, 16, 32, 128], P(('blk', 'wide'))
Inputs may be any that keep to these rules, and one draw needn't show every extreme that they name: `row_ids`: slot (d, b, c) names row d * 48 + value. `alt_ids`: slot (d, b, c) names centroid b * 8192 + value. The first counts[d, b] slots of device d toward owner b are live; one owner, the same on every device, gets 32 live slots from every device.
All inputs are finite; a program needn't handle non-finite values.
Results may differ from a plain program's by a relative error of at most 0.0003.
Values may be sent and summed in bfloat16 or wider, within the bound.
No kernel may reach another device: no remote copies, remote signals or barrier semaphores. Data moves between devices by JAX's collectives and lax.ppermute only.
A program may use at most 64 MiB of HBM per device.

v0:
```python
import math
import jax
import jax.numpy as jnp
from jax import lax
from jax.sharding import PartitionSpec as P

score_gain = 3.0


def local(tokens, centroids, row_ids, alt_ids, counts):
    scaling = score_gain / math.sqrt(tokens.shape[1])
    blk_count = lax.axis_size("blk")
    wide_count = lax.axis_size("wide")
    position = lax.axis_index("blk")
    tok_dev = tokens.shape[0]
    slab = centroids.shape[0]
    all_cols = slab * blk_count
    all_rows = tok_dev * blk_count * wide_count
    gathered = lax.all_gather(tokens, "blk", axis=0, tiled=True)
    group_rows = gathered.shape[0]
    block_cols = math.gcd(slab, 1024)
    col_blocks = centroids.reshape(slab // block_cols, block_cols, centroids.shape[1])

    def block_scores(centre_block):
        return (
            jnp.einsum("rd,kd->rk", gathered, centre_block, preferred_element_type=jnp.float32)
            * scaling
        )

    def online_step(carry, centre_block):
        running_peak, running_total = carry
        scores = block_scores(centre_block)
        new_peak = jnp.maximum(running_peak, jnp.max(scores, axis=1))
        new_total = running_total * jnp.exp(running_peak - new_peak) + jnp.sum(
            jnp.exp(scores - new_peak[:, None]), axis=1
        )
        return ((new_peak, new_total), None)

    initial = (
        jnp.full((group_rows,), -jnp.inf, jnp.float32),
        jnp.zeros((group_rows,), jnp.float32),
    )
    (local_peak, local_total), unused = lax.scan(online_step, initial, col_blocks)
    peak_score = lax.pmax(local_peak, "blk")
    totals = lax.psum(local_total * jnp.exp(local_peak - peak_score), "blk")
    row_group = math.log(all_cols) - (peak_score + jnp.log(totals))

    def block_mass(centre_block):
        scores = block_scores(centre_block)
        return jnp.sum(jnp.exp(scores + row_group[:, None]), axis=0)

    partial_mass = lax.map(block_mass, col_blocks).reshape(slab)
    col_duals = math.log(all_rows) - jnp.log(lax.psum(partial_mass, "wide"))
    row_duals = lax.dynamic_slice_in_dim(row_group, position * tok_dev, tok_dev)
    request_rows = row_ids[0]
    request_cols = alt_ids[0]
    capacity = request_rows.shape[1]
    live = (jnp.arange(capacity, dtype=jnp.int32)[None, :] < counts[0][:, None]).astype(jnp.int32)
    source_base = jnp.arange(blk_count, dtype=jnp.int32)[:, None] * tok_dev
    asked_rows = lax.all_to_all(request_rows, "blk", split_axis=0, concat_axis=0, tiled=True)
    asked_cols = lax.all_to_all(request_cols, "blk", split_axis=0, concat_axis=0, tiled=True)
    asked_live = lax.all_to_all(live, "blk", split_axis=0, concat_axis=0, tiled=True)
    rows_index = source_base + asked_rows
    picked = gathered[rows_index].astype(jnp.float32)
    centres = centroids[asked_cols].astype(jnp.float32)
    pair_scores = jnp.sum(picked * centres, axis=-1) * scaling
    picked, centres, weights = (
        picked,
        centres,
        jnp.exp(pair_scores + row_group[rows_index] + col_duals[asked_cols]),
    )
    weights = weights * asked_live.astype(jnp.float32)
    result = weights[..., None] * (picked - centres)
    residuals = lax.all_to_all(result, "blk", split_axis=0, concat_axis=0, tiled=True)
    return (row_duals, col_duals, residuals[None])


def solution(mesh):
    in_specs = (
        P(("blk", "wide"), None),
        P("blk", None),
        P(("blk", "wide"), None, None),
        P(("blk", "wide"), None, None),
        P(("blk", "wide"), None),
    )
    out_specs = (P(("blk", "wide")), P("blk"), P(("blk", "wide"), None, None, None))
    return jax.shard_map(local, mesh=mesh, in_specs=in_specs, out_specs=out_specs, check_vma=False)
```

profile of v0, /device:TPU:8, one launch (start us, length us, event | category | flops | bytes accessed | tf_op | source)
XLA Modules:
  0.0 324.0 jit_solution(13096027828668826560)
XLA Ops:
  0.6 9.4 %all-to-all-start = ((s32[16,1,32]{2,1,0:T(1,128)}), s32[16,1,32]{2,1,0:T(1,128)S(1)}, u32[]{:S(2)}, u32[]{:S(2)}) async-start(s32[16,1,32]{2,1,0:T(1,128)} %bitcast.48), calls=%async_computation | async-start | bytes 16384 | tf_op jit(solution)/shard_map/all_to_all | solution.py:60
  10.0 32.4 %all_gather.3 = bf16[768,128]{1,0:T(8,128)(2,1)S(1)} all-gather(bf16[48,128]{1,0:T(8,128)(2,1)} %param.9), channel_id=1, replica_groups=mesh['blk'=16,'wide'=32] {'blk'}, dimensions={0}, use_global_device_ids=true | all-gather | bytes 208896 | tf_op jit(solution)/shard_map/all_gather | solution.py:19
  42.4 17.3 %while.24 = (s32[]{:T(128)}, f32[768]{0:T(1024)S(1)}, f32[768]{0:T(1024)S(1)}, bf16[8,1024,128]{2,1,0:T(8,128)(2,1)}, bf16[768,128]{1,0:T(8,128)(2,1)S(1)}, /*index=5*/s32[]{:T(128)}, s32[]{:T(128)}) while((s32[]{:T(128)}, f32[768]{0:T(1024)S(1)}, f32[768]{0:T(1024)S(1)}, bf16[8,1024,128]{2,1,0:T(8,128)(2,1)}, ...), condition=%wide.region_3.4_spmd.clone, body=%wide.region_0.3_spmd.clone.sunk | while | flops 205262592 | bytes 6790244 | solution.py:43
  48.9 1.5 multiply_reduce_fusion.2
  59.7 30.6 %pmax.7 = f32[768]{0:T(1024)S(1)} all-reduce(f32[768]{0:T(1024)S(1)} %get-tuple-element.58), channel_id=1, replica_groups=mesh['blk'=16,'wide'=32] {'blk'}, use_global_device_ids=true, to_apply=%region_4.5 | all-reduce | flops 768 | bytes 6144 | tf_op jit(solution)/shard_map/pmax | solution.py:44
  90.3 32.6 %psum.14 = f32[768]{0:T(1024)S(1)} all-reduce(f32[768]{0:T(1024)S(1)} %exponential_multiply_fusion), channel_id=1, replica_groups=mesh['blk'=16,'wide'=32] {'blk'}, use_global_device_ids=true, to_apply=%region_5.6 | all-reduce | flops 768 | bytes 6144 | tf_op jit(solution)/shard_map/psum | solution.py:45
  123.0 14.5 %while.23 = (s32[]{:T(128)}, f32[8,1024]{1,0:T(8,128)S(1)}, bf16[8,1024,128]{2,1,0:T(8,128)(2,1)}, bf16[768,128]{1,0:T(8,128)(2,1)S(1)}, f32[768]{0:T(1024)S(1)}, /*index=5*/s32[]{:T(128)}, s32[]{:T(128)}) while((s32[]{:T(128)}, f32[8,1024]{1,0:T(8,128)S(1)}, bf16[8,1024,128]{2,1,0:T(8,128)(2,1)}, bf16[768,128]{1,0:T(8,128)(2,1)S(1)}, ...), condition=%wide.region_8.9_spmd, body=%wide.region_6.8_spmd.sunk | while | flops 203684864 | bytes 474205 | solution.py:52
  123.0 1.7 exponential_reduce_fusion.4
  124.8 1.7 exponential_reduce_fusion.4
  126.6 1.7 exponential_reduce_fusion.4
  128.4 1.7 exponential_reduce_fusion.4
  130.2 1.7 exponential_reduce_fusion.4
  132.0 1.7 exponential_reduce_fusion.4
  133.8 1.7 exponential_reduce_fusion.4
  135.6 1.7 exponential_reduce_fusion.4
  137.5 142.6 %psum.15 = f32[8192]{0:T(1024)S(1)} all-reduce(f32[8192]{0:T(1024)S(1)} %bitcast.42), channel_id=1, replica_groups=mesh['blk'=16,'wide'=32] {'wide'}, use_global_device_ids=true, to_apply=%region_9.10 | all-reduce | flops 8192 | bytes 65536 | tf_op jit(solution)/shard_map/psum | solution.py:53
  280.8 7.3 %all-to-all-start.1 = ((s32[16,1,32]{2,1,0:T(1,128)}), s32[16,1,32]{2,1,0:T(1,128)S(1)}, u32[]{:S(2)}, u32[]{:S(2)}) async-start(s32[16,1,32]{2,1,0:T(1,128)} %bitcast.5), calls=%async_computation.1 | async-start | bytes 16384 | tf_op jit(solution)/shard_map/all_to_all | solution.py:61
  289.6 2.3 gather_fusion.2
  291.9 3.3 %all-to-all-done.1 = s32[16,1,32]{2,1,0:T(1,128)S(1)} async-done(((s32[16,1,32]{2,1,0:T(1,128)}), s32[16,1,32]{2,1,0:T(1,128)S(1)}, u32[]{:S(2)}, u32[]{:S(2)}) %all-to-all-start.1) | async-done | bytes 2080 | tf_op jit(solution)/shard_map/all_to_all | solution.py:61
  295.2 4.9 %all-to-all-start.2 = ((s32[16,1,32]{2,1,0:T(1,128)}), s32[16,1,32]{2,1,0:T(1,128)S(1)}, u32[]{:S(2)}, u32[]{:S(2)}) async-start(s32[16,1,32]{2,1,0:T(1,128)} %compare_convert_fusion), calls=%async_computation.2 | async-start | bytes 16384 | tf_op jit(solution)/shard_map/all_to_all | solution.py:62
  301.5 3.1 gather_fusion.3
  304.9 2.2 all-to-all-done.2
  308.0 5.9 %all-to-all-start.3 = ((f32[16,32,128]{2,1,0:T(8,128)}), f32[16,32,128]{2,1,0:T(8,128)S(1)}, u32[]{:S(2)}, u32[]{:S(2)}) async-start(f32[16,32,128]{2,1,0:T(8,128)} %broadcast_multiply_fusion), calls=%async_computation.3 | async-start | bytes 524288 | tf_op jit(solution)/shard_map/all_to_all | solution.py:74
  314.5 8.8 %all-to-all-done.3 = f32[16,32,128]{2,1,0:T(8,128)S(1)} async-done(((f32[16,32,128]{2,1,0:T(8,128)}), f32[16,32,128]{2,1,0:T(8,128)S(1)}, u32[]{:S(2)}, u32[]{:S(2)}) %all-to-all-start.3) | async-done | bytes 262176 | tf_op jit(solution)/shard_map/all_to_all | solution.py:74
  (79 shorter events, 22.3 us)
Async XLA Ops:
  0.6 280.2 %all-to-all-start = ((s32[16,1,32]{2,1,0:T(1,128)}), s32[16,1,32]{2,1,0:T(1,128)S(1)}, u32[]{:S(2)}, u32[]{:S(2)}) async-start(s32[16,1,32]{2,1,0:T(1,128)} %bitcast.48), calls=%async_computation | async-start | bytes 16384 | tf_op jit(solution)/shard_map/all_to_all | solution.py:60
  123.0 157.2 %copy-start.2 = (s32[1,16]{1,0:T(1,128)S(1)}, s32[1,16]{1,0:T(1,128)}, u32[]{:S(2)}) copy-start(s32[1,16]{1,0:T(1,128)} %param.13) | copy-start | bytes 196
  280.1 21.4 %copy-start = (f32[8192]{0:T(1024)}, f32[8192]{0:T(1024)S(1)}, u32[]{:S(2)}) copy-start(f32[8192]{0:T(1024)S(1)} %log_subtract_fusion) | copy-start | bytes 98308
  280.8 14.4 %all-to-all-start.1 = ((s32[16,1,32]{2,1,0:T(1,128)}), s32[16,1,32]{2,1,0:T(1,128)S(1)}, u32[]{:S(2)}, u32[]{:S(2)}) async-start(s32[16,1,32]{2,1,0:T(1,128)} %bitcast.5), calls=%async_computation.1 | async-start | bytes 16384 | tf_op jit(solution)/shard_map/all_to_all | solution.py:61
  289.6 10.6 %copy-start.1 = (bf16[8,1024,128]{2,1,0:T(8,128)(2,1)S(1)}, bf16[8,1024,128]{2,1,0:T(8,128)(2,1)}, u32[]{:S(2)}) copy-start(bf16[8,1024,128]{2,1,0:T(8,128)(2,1)} %get-tuple-element.221) | copy-start | bytes 6291460
  295.2 12.0 %all-to-all-start.2 = ((s32[16,1,32]{2,1,0:T(1,128)}), s32[16,1,32]{2,1,0:T(1,128)S(1)}, u32[]{:S(2)}, u32[]{:S(2)}) async-start(s32[16,1,32]{2,1,0:T(1,128)} %compare_convert_fusion), calls=%async_computation.2 | async-start | bytes 16384 | tf_op jit(solution)/shard_map/all_to_all | solution.py:62
  308.0 15.3 %all-to-all-start.3 = ((f32[16,32,128]{2,1,0:T(8,128)}), f32[16,32,128]{2,1,0:T(8,128)S(1)}, u32[]{:S(2)}, u32[]{:S(2)}) async-start(f32[16,32,128]{2,1,0:T(8,128)} %broadcast_multiply_fusion), calls=%async_computation.3 | async-start | bytes 524288 | tf_op jit(solution)/shard_map/all_to_all | solution.py:74
where the time goes:
time: 325 us; the launch traced here: 324 us
  blocking collectives  238 us (73%)
  starting transfers between devices  27.5 us (8%)
  matrix products  25.6 us (8%)
  waiting for transfers between devices  14.3 us (4%)
  local copies, waits for them, and re-layouts  10.5 us (3%)
  other arithmetic  6.47 us (2%)
    psum x1, blocking collectives, local(): col_duals = math.log(all_rows) - jnp.log(lax.psum(partial_mass, 'wide'))  143 us
    psum x1, blocking collectives, local(): totals = lax.psum(local_total * jnp.exp(local_peak - peak_score), 'blk')  32.6 us
    all_gather x1, blocking collectives, local(): gathered = lax.all_gather(tokens, 'blk', axis=0, tiled=True)  32.4 us
    pmax x1, blocking collectives, local(): peak_score = lax.pmax(local_peak, 'blk')  30.6 us
    dot_general x16, matrix products, block_scores(): jnp.einsum('rd,kd->rk', gathered, centre_block, preferred_element_type=jn...  25.6 us
    all_to_all x1, starting transfers between devices, local(): lax.all_to_all(request_rows, 'blk', split_axis=0, concat_axis=0, tiled=True)  9.38 us
    all_to_all x1, waiting for transfers between devices, local(): lax.all_to_all(result, 'blk', split_axis=0, concat_axis=0, tiled=True)  8.82 us
    all_to_all x1, starting transfers between devices, local(): lax.all_to_all(request_cols, 'blk', split_axis=0, concat_axis=0, tiled=True)  7.3 us
  transfers between devices with their start and end apart: 4, of which 3 were waited for; matrix products, arithmetic and copies ran while one was open for 13% of the time, Pallas kernels for 0%

commit v1 on v0

--- a/solution.py
+++ b/solution.py
@@ -3,8 +3,14 @@
 import jax.numpy as jnp
 from jax import lax
 from jax.sharding import PartitionSpec as P
+from jax.lax import all_gather
 
 score_gain = 3.0
+
+
+def do_the_slots(vec):
+    b_next = all_gather(vec, "wide").sum(axis=0)
+    return b_next
 
 
 def local(tokens, centroids, row_ids, alt_ids, counts):
@@ -50,7 +56,7 @@
         return jnp.sum(jnp.exp(scores + row_group[:, None]), axis=0)
 
     partial_mass = lax.map(block_mass, col_blocks).reshape(slab)
-    col_duals = math.log(all_rows) - jnp.log(lax.psum(partial_mass, "wide"))
+    col_duals = math.log(all_rows) - jnp.log(do_the_slots(partial_mass))
     row_duals = lax.dynamic_slice_in_dim(row_group, position * tok_dev, tok_dev)
     request_rows = row_ids[0]
     request_cols = alt_ids[0]

time: 325 us -> 231 us (0.71)
  the two profiles are of different devices: /device:TPU:8 before, /device:TPU:1 now
where the time goes in v1:
time: 231 us
  blocking collectives  78.9 us (34%)
  waiting for transfers between devices  74.1 us (32%)
  matrix products  25.5 us (11%)
  starting transfers between devices  17.7 us (8%)
  between operations  14.2 us (6%)
  local copies, waits for them, and re-layouts  11.2 us (5%)
  other arithmetic  8.39 us (4%)
    all_gather x1, waiting for transfers between devices, do_the_slots(): b_next = all_gather(vec, 'wide').sum(axis=0)  47.8 us
    all_gather x1, blocking collectives, local(): gathered = lax.all_gather(tokens, 'blk', axis=0, tiled=True)  30 us
    dot_general x16, matrix products, block_scores(): jnp.einsum('rd,kd->rk', gathered, centre_block, preferred_element_type=jn...  25.5 us
    psum x1, blocking collectives, local(): totals = lax.psum(local_total * jnp.exp(local_peak - peak_score), 'blk')  25.2 us
    pmax x1, blocking collectives, local(): peak_score = lax.pmax(local_peak, 'blk')  23.7 us
    all_to_all x1, waiting for transfers between devices, local(): lax.all_to_all(result, 'blk', split_axis=0, concat_axis=0, tiled=True)  10.6 us
    all_to_all x1, waiting for transfers between devices, local(): lax.all_to_all(request_rows, 'blk', split_axis=0, concat_axis=0, tiled=True)  7.12 us
    all_to_all x1, waiting for transfers between devices, local(): lax.all_to_all(request_cols, 'blk', split_axis=0, concat_axis=0, tiled=True)  6.58 us
  transfers between devices with their start and end apart: 5, of which 5 were waited for; matrix products, arithmetic and copies ran while one was open for 3% of the time, Pallas kernels for 0%

profile of v1, /device:TPU:1, one launch (start us, length us, event | category | flops | bytes accessed | tf_op | source)
XLA Modules:
  0.0 230.5 jit_solution(13576784273176919774)
XLA Ops:
  7.2 30.0 %all_gather.6 = bf16[768,128]{1,0:T(8,128)(2,1)S(1)} all-gather(bf16[48,128]{1,0:T(8,128)(2,1)} %param.9), channel_id=1, replica_groups=mesh['blk'=16,'wide'=32] {'blk'}, dimensions={0}, use_global_device_ids=true | all-gather | bytes 208896 | tf_op jit(solution)/shard_map/all_gather | solution.py:25
  37.2 17.2 %while.24 = (s32[]{:T(128)}, f32[768]{0:T(1024)S(1)}, f32[768]{0:T(1024)S(1)}, bf16[8,1024,128]{2,1,0:T(8,128)(2,1)}, bf16[768,128]{1,0:T(8,128)(2,1)S(1)}, /*index=5*/s32[]{:T(128)}, s32[]{:T(128)}) while((s32[]{:T(128)}, f32[768]{0:T(1024)S(1)}, f32[768]{0:T(1024)S(1)}, bf16[8,1024,128]{2,1,0:T(8,128)(2,1)}, ...), condition=%wide.region_3.4_spmd.clone, body=%wide.region_0.3_spmd.clone.sunk | while | flops 205262592 | bytes 6790244 | solution.py:49
  54.4 23.7 %pmax.7 = f32[768]{0:T(1024)S(1)} all-reduce(f32[768]{0:T(1024)S(1)} %get-tuple-element.58), channel_id=1, replica_groups=mesh['blk'=16,'wide'=32] {'blk'}, use_global_device_ids=true, to_apply=%region_4.5 | all-reduce | flops 768 | bytes 6144 | tf_op jit(solution)/shard_map/pmax | solution.py:50
  78.1 25.2 %psum.7 = f32[768]{0:T(1024)S(1)} all-reduce(f32[768]{0:T(1024)S(1)} %exponential_multiply_fusion), channel_id=1, replica_groups=mesh['blk'=16,'wide'=32] {'blk'}, use_global_device_ids=true, to_apply=%region_5.6 | all-reduce | flops 768 | bytes 6144 | tf_op jit(solution)/shard_map/psum | solution.py:51
  103.4 14.4 %while.23 = (s32[]{:T(128)}, f32[8,1024]{1,0:T(8,128)S(1)}, bf16[8,1024,128]{2,1,0:T(8,128)(2,1)}, bf16[768,128]{1,0:T(8,128)(2,1)S(1)}, f32[768]{0:T(1024)S(1)}, /*index=5*/s32[]{:T(128)}, s32[]{:T(128)}) while((s32[]{:T(128)}, f32[8,1024]{1,0:T(8,128)S(1)}, bf16[8,1024,128]{2,1,0:T(8,128)(2,1)}, bf16[768,128]{1,0:T(8,128)(2,1)S(1)}, ...), condition=%wide.region_8.9_spmd, body=%wide.region_6.8_spmd.sunk | while | flops 203684864 | bytes 474205 | solution.py:58
  103.4 1.7 exponential_reduce_fusion.4
  105.2 1.7 exponential_reduce_fusion.4
  107.0 1.7 exponential_reduce_fusion.4
  108.8 1.7 exponential_reduce_fusion.4
  110.6 1.7 exponential_reduce_fusion.4
  112.4 1.7 exponential_reduce_fusion.4
  116.0 1.7 exponential_reduce_fusion.4
  118.4 4.1 %all-to-all-start.1 = ((s32[16,1,32]{2,1,0:T(1,128)}), s32[16,1,32]{2,1,0:T(1,128)S(1)}, u32[]{:S(2)}, u32[]{:S(2)}) async-start(s32[16,1,32]{2,1,0:T(1,128)} %bitcast.5), calls=%async_computation.1 | async-start | bytes 16384 | tf_op jit(solution)/shard_map/all_to_all | solution.py:67
  123.3 6.6 %all-to-all-done.1 = s32[16,1,32]{2,1,0:T(1,128)S(1)} async-done(((s32[16,1,32]{2,1,0:T(1,128)}), s32[16,1,32]{2,1,0:T(1,128)S(1)}, u32[]{:S(2)}, u32[]{:S(2)}) %all-to-all-start.1) | async-done | bytes 2080 | tf_op jit(solution)/shard_map/all_to_all | solution.py:67
  129.8 3.5 %all-to-all-start = ((s32[16,1,32]{2,1,0:T(1,128)}), s32[16,1,32]{2,1,0:T(1,128)S(1)}, u32[]{:S(2)}, u32[]{:S(2)}) async-start(s32[16,1,32]{2,1,0:T(1,128)} %bitcast.3), calls=%async_computation | async-start | bytes 16384 | tf_op jit(solution)/shard_map/all_to_all | solution.py:66
  133.4 7.1 %all-to-all-done = s32[16,1,32]{2,1,0:T(1,128)S(1)} async-done(((s32[16,1,32]{2,1,0:T(1,128)}), s32[16,1,32]{2,1,0:T(1,128)S(1)}, u32[]{:S(2)}, u32[]{:S(2)}) %all-to-all-start) | async-done | bytes 2080 | tf_op jit(solution)/shard_map/all_to_all | solution.py:66
  140.5 3.5 %all-to-all-start.2 = ((s32[16,1,32]{2,1,0:T(1,128)}), s32[16,1,32]{2,1,0:T(1,128)S(1)}, u32[]{:S(2)}, u32[]{:S(2)}) async-start(s32[16,1,32]{2,1,0:T(1,128)} %compare_convert_fusion), calls=%async_computation.2 | async-start | bytes 16384 | tf_op jit(solution)/shard_map/all_to_all | solution.py:68
  145.5 2.3 gather_fusion.2
  149.2 2.0 all-to-all-done.2
  151.4 47.8 %all-gather.3.cloned.1.call-done = f32[32,1,8192]{2,1,0:T(1,128)} async-done(((f32[1,1,8192]{2,1,0:T(1,128)}), f32[32,1,8192]{2,1,0:T(1,128)}) %all-gather.3.cloned.1.call-update) | async-done | bytes 1048592 | tf_op jit(solution)/shard_map/all_gather | solution.py:12
  199.2 1.9 reduce_sum.36
  201.1 3.1 %gather_fusion.3 = f32[512]{0:T(512)S(1)} fusion(f32[8192]{0:T(1024)S(1)} %log_subtract_fusion, s32[1024]{0:T(1024)S(1)} %pad_clamp_fusion), kind=kCustom, calls=%fused_computation.3 | custom fusion | bytes 6144 | tf_op jit(solution)/shard_map/gather | solution.py:76
  205.2 6.6 %all-to-all-start.3 = ((f32[16,32,128]{2,1,0:T(8,128)}), f32[16,32,128]{2,1,0:T(8,128)S(1)}, u32[]{:S(2)}, u32[]{:S(2)}) async-start(f32[16,32,128]{2,1,0:T(8,128)} %broadcast_multiply_fusion), calls=%async_computation.3 | async-start | bytes 524288 | tf_op jit(solution)/shard_map/all_to_all | solution.py:80
  212.4 10.6 %all-to-all-done.3 = f32[16,32,128]{2,1,0:T(8,128)S(1)} async-done(((f32[16,32,128]{2,1,0:T(8,128)}), f32[16,32,128]{2,1,0:T(8,128)S(1)}, u32[]{:S(2)}, u32[]{:S(2)}) %all-to-all-start.3) | async-done | bytes 262176 | tf_op jit(solution)/shard_map/all_to_all | solution.py:80
  (82 shorter events, 26.2 us)
Async XLA Ops:
  7.2 192.0 %all-gather.3.cloned.1.call-start = ((), (), s32[]{:S(2)}) async-start(), calls=%async_computation.4 | async-start | bytes 1081344 | tf_op jit(solution)/shard_map/all_gather | solution.py:12
  103.4 19.2 %copy-start.2 = (s32[1,16]{1,0:T(1,128)S(1)}, s32[1,16]{1,0:T(1,128)}, u32[]{:S(2)}) copy-start(s32[1,16]{1,0:T(1,128)} %param.13) | copy-start | bytes 196
  118.4 11.4 %all-to-all-start.1 = ((s32[16,1,32]{2,1,0:T(1,128)}), s32[16,1,32]{2,1,0:T(1,128)S(1)}, u32[]{:S(2)}, u32[]{:S(2)}) async-start(s32[16,1,32]{2,1,0:T(1,128)} %bitcast.5), calls=%async_computation.1 | async-start | bytes 16384 | tf_op jit(solution)/shard_map/all_to_all | solution.py:67
  129.8 10.7 %all-to-all-start = ((s32[16,1,32]{2,1,0:T(1,128)}), s32[16,1,32]{2,1,0:T(1,128)S(1)}, u32[]{:S(2)}, u32[]{:S(2)}) async-start(s32[16,1,32]{2,1,0:T(1,128)} %bitcast.3), calls=%async_computation | async-start | bytes 16384 | tf_op jit(solution)/shard_map/all_to_all | solution.py:66
  140.5 10.7 %all-to-all-start.2 = ((s32[16,1,32]{2,1,0:T(1,128)}), s32[16,1,32]{2,1,0:T(1,128)S(1)}, u32[]{:S(2)}, u32[]{:S(2)}) async-start(s32[16,1,32]{2,1,0:T(1,128)} %compare_convert_fusion), calls=%async_computation.2 | async-start | bytes 16384 | tf_op jit(solution)/shard_map/all_to_all | solution.py:68
  145.5 2.3 %copy-start.1 = (bf16[8,1024,128]{2,1,0:T(8,128)(2,1)S(1)}, bf16[8,1024,128]{2,1,0:T(8,128)(2,1)}, u32[]{:S(2)}) copy-start(bf16[8,1024,128]{2,1,0:T(8,128)(2,1)} %get-tuple-element.222) | copy-start | bytes 6291460
  201.1 3.2 %copy-start = (f32[8192]{0:T(1024)}, f32[8192]{0:T(1024)S(1)}, u32[]{:S(2)}) copy-start(f32[8192]{0:T(1024)S(1)} %log_subtract_fusion) | copy-start | bytes 98308
  205.2 17.7 %all-to-all-start.3 = ((f32[16,32,128]{2,1,0:T(8,128)}), f32[16,32,128]{2,1,0:T(8,128)S(1)}, u32[]{:S(2)}, u32[]{:S(2)}) async-start(f32[16,32,128]{2,1,0:T(8,128)} %broadcast_multiply_fusion), calls=%async_computation.3 | async-start | bytes 524288 | tf_op jit(solution)/shard_map/all_to_all | solution.py:80
Sparse Core Ops, SparseCore 0:
  118.6 80.5 all-gather.2
